TPU v7x, 256 devices: a whole 4x4x8 slice. The times are simulated.
256 devices in a mesh: segment: 8 (over y, z_lo), frame: 32 (over x, z_hi, core).
Axes of the slice: x: 4, y: 4, z: 8 (z_hi: 4, z_lo: 2; z = z_hi * 2 + z_lo), core: 2. Of those that a mesh axis runs over, the one named last changes fastest.
Arguments:
- noisy_clips: bfloat16 [4, 32, 16, 16, 512], P(None, 'frame'), may hold values from -6 to 6
- conv_first: bfloat16 [8, 9, 512, 512], P('segment', None, 'frame'), may hold values from -0.09375 to 0.09375
- conv_second: bfloat16 [8, 9, 512, 512], P('segment', None, 'frame'), may hold values from -0.09375 to 0.09375
- temporal: bfloat16 [8, 3, 512, 512], P('segment', None, 'frame'), may hold values from -0.15625 to 0.15625
Outputs:
- denoised: bfloat16 [4, 32, 16, 16, 512], P(None, 'frame', 'segment')
All inputs are finite; a program needn't handle non-finite values.
Results may differ from a plain program's by a relative error of at most 0.013.
Values may be sent and summed in bfloat16 or wider, within the bound.
No kernel may reach another device: no remote copies, remote signals or barrier semaphores. Data moves between devices by JAX's collectives and lax.ppermute only.
A program may use at most 64 MiB of HBM per device.

v0:
```python
import jax
import jax.numpy as jnp
from jax import lax
from jax.sharding import PartitionSpec as P

skip_scale = 0.7071067811865476


def passed_along(shard, axis, by):
    length = lax.axis_size(axis)
    pairs = [(i, i + by) for i in range(length) if 0 <= i + by < length]
    return lax.ppermute(shard, axis, pairs)


def partner(shard, axis, bit):
    return lax.ppermute(shard, axis, [(i, i ^ 1 << bit) for i in range(lax.axis_size(axis))])


def extended_2(cells, sides, width):
    for axis, dim in sides:
        count = lax.axis_size(axis)
        ends = count - 1
        head = lax.slice_in_dim(cells, 0, width, axis=dim)
        tail = lax.slice_in_dim(cells, cells.shape[dim] - width, cells.shape[dim], axis=dim)
        cells = jnp.concatenate(
            [
                lax.ppermute(tail, axis, [(i, (i + 1) % count) for i in range(ends)]),
                cells,
                lax.ppermute(head, axis, [((i + 1) % count, i) for i in range(ends)]),
            ],
            axis=dim,
        )
    return cells


def broadcast(shard, axis, root):
    mine = lax.axis_index(axis) == root
    return lax.psum(jnp.where(mine, shard, jnp.zeros_like(shard)), axis)


def spatial(field_in, kernel):
    extent = field_in.shape[1]
    channels = field_in.shape[3]
    padded = jnp.pad(field_in, ((0, 0), (1, 1), (1, 1), (0, 0)))
    accumulated = jnp.zeros((field_in.shape[0] * extent * extent, channels), jnp.float32)
    for row_shift in range(3):
        for col_shift in range(3):
            window = padded[
                :, row_shift : row_shift + extent, col_shift : col_shift + extent, :
            ].reshape(-1, channels)
            accumulated = accumulated + jnp.dot(
                window, kernel[3 * row_shift + col_shift], preferred_element_type=jnp.float32
            )
    return accumulated.reshape(field_in.shape)


def temporal_mix(extended, kernel, frame_local):
    channels = extended.shape[3]
    out_shape = (frame_local,) + extended.shape[1:]
    accumulated = jnp.zeros(out_shape, jnp.float32)
    for offset in range(3):
        window = extended[offset : offset + frame_local].reshape(-1, channels)
        accumulated = accumulated + jnp.dot(
            window, kernel[offset], preferred_element_type=jnp.float32
        ).reshape(out_shape)
    return accumulated


def on_device(noisy_clips, conv_first, conv_second, temporal):
    sections = lax.axis_size("segment")
    segment_id = lax.axis_index("segment")
    first_full, second_full, time_full = (
        lax.all_gather(conv_first, "frame", axis=2, tiled=True),
        lax.all_gather(conv_second, "frame", axis=2, tiled=True),
        lax.all_gather(temporal, "frame", axis=2, tiled=True),
    )
    first_kernel = first_full[0]
    second_kernel = second_full[0]
    time_kernel = time_full[0]
    clip_count = noisy_clips.shape[0]
    frame_local = noisy_clips.shape[1]
    side_len = noisy_clips.shape[2]
    block_shape = noisy_clips.shape[1:]
    tick_count = clip_count + sections - 1
    half_sections = sections // 2
    is_up = segment_id >= half_sections
    side_store = jnp.zeros((clip_count,) + block_shape, jnp.bfloat16)
    out_store = jnp.zeros(noisy_clips.shape, jnp.bfloat16)
    prev_out = jnp.zeros(block_shape, jnp.bfloat16)

    def tick_step(carry, tick_index):
        prev_out, side_store, out_store = carry
        clip_now = tick_index - segment_id
        active = (clip_now >= 0) & (clip_now < clip_count)
        clip_slot = jnp.clip(clip_now, 0, clip_count - 1)
        own_input = lax.dynamic_index_in_dim(noisy_clips, clip_slot, 0, keepdims=False)
        received = passed_along(prev_out, "segment", 1)
        entering = jnp.where(segment_id == 0, own_input, received)
        mirrored = entering
        for bit_number in range(sections.bit_length() - 1):
            mirrored = partner(mirrored, "segment", bit_number)
        mirror_clip = tick_index - (sections - 1 - segment_id)
        written = (jnp.arange(clip_count) == mirror_clip) & is_up
        side_store = jnp.where(written[:, None, None, None, None], mirrored[None], side_store)
        skip_feature = lax.dynamic_index_in_dim(side_store, clip_slot, 0, keepdims=False)
        joined = (
            (entering.astype(jnp.float32) + skip_feature.astype(jnp.float32)) * skip_scale
        ).astype(jnp.bfloat16)
        section_in = jnp.where(is_up, joined, entering)
        activated = lax.cond(
            active,
            lambda: jax.nn.silu(spatial(section_in, first_kernel)).astype(jnp.bfloat16),
            lambda: jnp.zeros(block_shape, jnp.bfloat16),
        )
        extended = extended_2(activated, (("frame", 0),), 1)

        def second_pass():
            branch_sum = spatial(activated, second_kernel) + temporal_mix(
                extended, time_kernel, frame_local
            )
            return (section_in.astype(jnp.float32) + jax.nn.silu(branch_sum)).astype(jnp.bfloat16)

        section_out = lax.cond(active, second_pass, lambda: jnp.zeros(block_shape, jnp.bfloat16))
        finished = (jnp.arange(clip_count) == clip_slot) & active & (segment_id == sections - 1)
        out_store = jnp.where(finished[:, None, None, None, None], section_out[None], out_store)
        return ((section_out, side_store, out_store), None)

    final_carry, unused = lax.scan(
        tick_step, (prev_out, side_store, out_store), jnp.arange(tick_count, dtype=jnp.int32)
    )
    delivered = broadcast(final_carry[2], "segment", sections - 1)
    slab_rows = side_len // sections
    return lax.dynamic_slice_in_dim(delivered, segment_id * slab_rows, slab_rows, 2)


def solution(mesh):
    in_specs = (
        P(None, "frame", None, None, None),
        P("segment", None, "frame", None),
        P("segment", None, "frame", None),
        P("segment", None, "frame", None),
    )
    out_specs = P(None, "frame", "segment", None, None)
    return jax.shard_map(
        on_device, mesh=mesh, in_specs=in_specs, out_specs=out_specs, check_vma=False
    )
```

profile of v0, /device:TPU:2, one launch (start us, length us, event | category | flops | bytes accessed | tf_op | source)
XLA Modules:
  0.0 975.8 jit_solution(13421447813197799213)
XLA Ops:
  8.8 56.3 %all-gather.8.cloned.1.call-done = bf16[1,3,512,512]{3,2,1,0:T(8,128)(2,1)} async-done(((bf16[1,3,16,512]{3,2,1,0:T(8,128)(2,1)}), bf16[1,3,512,512]{3,2,1,0:T(8,128)(2,1)}) %all-gather.8.cloned.1.call-update) | async-done | bytes 1572880 | tf_op jit(solution)/shard_map/all_gather | solution.py:75
  65.1 63.4 %all-gather.4.cloned.1.call-done = bf16[1,9,512,512]{3,2,1,0:T(8,128)(2,1)} async-done(((bf16[1,9,16,512]{3,2,1,0:T(8,128)(2,1)}), bf16[1,9,512,512]{3,2,1,0:T(8,128)(2,1)}) %all-gather.4.cloned.1.call-update) | async-done | bytes 4718608 | tf_op jit(solution)/shard_map/all_gather | solution.py:73
  128.4 63.1 %all-gather.6.cloned.1.call-done = bf16[1,9,512,512]{3,2,1,0:T(8,128)(2,1)} async-done(((bf16[1,9,16,512]{3,2,1,0:T(8,128)(2,1)}), bf16[1,9,512,512]{3,2,1,0:T(8,128)(2,1)}) %all-gather.6.cloned.1.call-update) | async-done | bytes 4718608 | tf_op jit(solution)/shard_map/all_gather | solution.py:74
  192.3 682.3 %while.16 = (s32[]{:T(128)}, bf16[1,16,16,512]{3,2,1,0:T(8,128)(2,1)}, bf16[4,1,16,16,512]{4,3,2,1,0:T(8,128)(2,1)S(1)}, bf16[4,1,16,16,512]{4,3,2,1,0:T(8,128)(...) while((s32[]{:T(128)}, ...), condition=%wide.region_5.6_spmd.clone, body=%wide.region_0.5_spmd.clone.sunk | while | flops 2825650176 | bytes 99615424 | solution.py:128
  204.5 5.9 collective-permute-done.1
  234.9 6.7 collective-permute-start.5
  245.5 7.0 conditional.7
  264.7 5.8 collective-permute-done.1
  270.5 7.6 collective-permute-done.2
  278.8 7.2 collective-permute-done.3
  293.9 6.7 collective-permute-start.5
  307.3 7.0 conditional.7
  327.6 6.3 collective-permute-done.1
  335.6 5.7 collective-permute-done.2
  342.1 7.3 collective-permute-done.3
  357.3 6.7 collective-permute-start.5
  370.6 7.0 conditional.7
  390.7 6.3 collective-permute-done.1
  397.8 7.7 collective-permute-done.2
  406.1 7.2 collective-permute-done.3
  421.2 6.7 collective-permute-start.5
  434.5 7.0 conditional.7
  452.0 6.5 collective-permute-done.1
  462.1 5.7 collective-permute-done.2
  468.4 7.5 collective-permute-done.3
  478.5 6.7 collective-permute-start.5
  491.1 14.6 %collective-permute-start = (bf16[1,16,16,512]{3,2,1,0:T(8,128)(2,1)}, bf16[1,16,16,512]{3,2,1,0:T(8,128)(2,1)S(1)}, u32[]{:S(2)}, u32[]{:S(2)}) collective-permute-start(bf16[1,16,16,512]{3,2,1,0:T(8,128)(2,1)} %get-tuple-element.343), channel_id=1, source_target_pairs={{0,32},{32,64},{64,96},{96,128},{128,160},{160,192},{192,224},{1,3... | collective-permute-start | bytes 786440 | tf_op jit(solution)/shard_map/while/body/eval_jaxpr/ppermute | solution.py:12
  510.8 6.9 collective-permute-start.1
  531.0 7.2 collective-permute-done.3
  540.6 6.7 collective-permute-start.5
  562.9 15.2 %collective-permute-start.1 = (bf16[1,16,16,512]{3,2,1,0:T(8,128)(2,1)S(1)}, bf16[1,16,16,512]{3,2,1,0:T(8,128)(2,1)S(1)}, u32[]{:S(2)}, u32[]{:S(2)}) collective-permute-start(bf16[1,16,16,512]{3,2,1,0:T(8,128)(2,1)S(1)} %bitcast_select_fusion.2), channel_id=1, source_target_pairs={{0,32},{32,0},{64,96},{96,64},{128,160},{160,128},{192,224},{224,1... | collective-permute-start | bytes 786440 | tf_op jit(solution)/shard_map/while/body/eval_jaxpr/ppermute | solution.py:16
  578.1 6.3 collective-permute-done.1
  594.0 7.3 collective-permute-done.3
  603.8 6.7 collective-permute-start.5
  631.9 6.0 collective-permute-done.1
  637.9 11.0 %collective-permute-start.2 = (bf16[1,16,16,512]{3,2,1,0:T(8,128)(2,1)S(1)}, bf16[1,16,16,512]{3,2,1,0:T(8,128)(2,1)S(1)}, u32[]{:S(2)}, u32[]{:S(2)}) collective-permute-start(bf16[1,16,16,512]{3,2,1,0:T(8,128)(2,1)S(1)} %collective-permute-done.1), channel_id=1, source_target_pairs={{0,64},{32,96},{64,0},{96,32},{128,192},{160,224},{192,128},{224,1... | collective-permute-start | bytes 786440 | tf_op jit(solution)/shard_map/while/body/eval_jaxpr/ppermute | solution.py:16
  648.8 5.9 collective-permute-done.2
  666.8 6.7 collective-permute-start.5
  699.2 13.0 %collective-permute-start.2 = (bf16[1,16,16,512]{3,2,1,0:T(8,128)(2,1)S(1)}, bf16[1,16,16,512]{3,2,1,0:T(8,128)(2,1)S(1)}, u32[]{:S(2)}, u32[]{:S(2)}) collective-permute-start(bf16[1,16,16,512]{3,2,1,0:T(8,128)(2,1)S(1)} %collective-permute-done.1), channel_id=1, source_target_pairs={{0,64},{32,96},{64,0},{96,32},{128,192},{160,224},{192,128},{224,1... | collective-permute-start | bytes 786440 | tf_op jit(solution)/shard_map/while/body/eval_jaxpr/ppermute | solution.py:16
  716.5 6.2 collective-permute-start.3
  729.6 6.7 collective-permute-start.5
  767.6 19.2 %collective-permute-start.3 = (bf16[1,16,16,512]{3,2,1,0:T(8,128)(2,1)S(1)}, bf16[1,16,16,512]{3,2,1,0:T(8,128)(2,1)S(1)}, u32[]{:S(2)}, u32[]{:S(2)}) collective-permute-start(bf16[1,16,16,512]{3,2,1,0:T(8,128)(2,1)S(1)} %collective-permute-done.2), channel_id=1, source_target_pairs={{0,128},{32,160},{64,192},{96,224},{128,0},{160,32},{192,64},{224,... | collective-permute-start | bytes 786440 | tf_op jit(solution)/shard_map/while/body/eval_jaxpr/ppermute | solution.py:16
  793.6 6.7 collective-permute-start.5
  820.8 5.9 collective-permute-done.1
  829.7 6.2 collective-permute-done.2
  835.9 15.5 %collective-permute-start.3 = (bf16[1,16,16,512]{3,2,1,0:T(8,128)(2,1)S(1)}, bf16[1,16,16,512]{3,2,1,0:T(8,128)(2,1)S(1)}, u32[]{:S(2)}, u32[]{:S(2)}) collective-permute-start(bf16[1,16,16,512]{3,2,1,0:T(8,128)(2,1)S(1)} %collective-permute-done.2), channel_id=1, source_target_pairs={{0,128},{32,160},{64,192},{96,224},{128,0},{160,32},{192,64},{224,... | collective-permute-start | bytes 786440 | tf_op jit(solution)/shard_map/while/body/eval_jaxpr/ppermute | solution.py:16
  859.2 6.7 collective-permute-start.5
  875.7 92.0 %all-reduce.4.cloned.1.call-done = bf16[4,1,16,16,512]{4,3,2,1,0:T(8,128)(2,1)} async-done(((bf16[4,1,16,16,512]{4,3,2,1,0:T(8,128)(2,1)}), bf16[4,1,16,16,512]{4,3,2,1,0:T(8,128)(2,1)}) %all-reduce.4.cloned.1.call-update) | async-done | bytes 1048592 | tf_op jit(solution)/shard_map/psum | solution.py:38
  (336 shorter events, 391.8 us)
Async XLA Ops:
  6.5 58.5 %all-gather.8.cloned.1.call-start = ((), (), s32[]{:S(2)}) async-start(), calls=%async_computation.2 | async-start | bytes 1622016 | tf_op jit(solution)/shard_map/all_gather | solution.py:75
  7.3 121.2 %all-gather.4.cloned.1.call-start = ((), (), s32[]{:S(2)}) async-start(), calls=%async_computation | async-start | bytes 4866048 | tf_op jit(solution)/shard_map/all_gather | solution.py:73
  8.0 183.6 %all-gather.6.cloned.1.call-start = ((), (), s32[]{:S(2)}) async-start(), calls=%async_computation.1 | async-start | bytes 4866048 | tf_op jit(solution)/shard_map/all_gather | solution.py:74
  8.7 959.0 %all-reduce.4.cloned.1.call-start = ((), (), s32[]{:S(2)}) async-start(), calls=%async_computation.3 | async-start | bytes 2097152 | tf_op jit(solution)/shard_map/psum | solution.py:38
  201.1 9.3 collective-permute-start.1
  210.4 8.6 collective-permute-start.2
  233.0 10.7 %collective-permute-start.4 = (bf16[1,16,16,512]{3,2,1,0:T(8,128)(2,1)S(1)}, bf16[1,16,16,512]{3,2,1,0:T(8,128)(2,1)S(1)}, u32[]{:S(2)}, u32[]{:S(2)}) collective-permute-start(bf16[1,16,16,512]{3,2,1,0:T(8,128)(2,1)S(1)} %get-tuple-element.378), channel_id=1, source_target_pairs={{0,1},{1,2},{2,3},{3,4},{4,5},{5,6},{6,7},{7,8},{8,9},{9,10},{10,1... | collective-permute-start | bytes 786440 | tf_op jit(solution)/shard_map/while/body/eval_jaxpr/ppermute | solution.py:27
  234.9 10.5 %collective-permute-start.5 = (bf16[1,16,16,512]{3,2,1,0:T(8,128)(2,1)S(1)}, bf16[1,16,16,512]{3,2,1,0:T(8,128)(2,1)S(1)}, u32[]{:S(2)}, u32[]{:S(2)}) collective-permute-start(bf16[1,16,16,512]{3,2,1,0:T(8,128)(2,1)S(1)} %get-tuple-element.378), channel_id=1, source_target_pairs={{1,0},{2,1},{3,2},{4,3},{5,4},{6,5},{7,6},{8,7},{9,8},{10,9},{11,1... | collective-permute-start | bytes 786440 | tf_op jit(solution)/shard_map/while/body/eval_jaxpr/ppermute | solution.py:29
  292.0 10.9 %collective-permute-start.4 = (bf16[1,16,16,512]{3,2,1,0:T(8,128)(2,1)S(1)}, bf16[1,16,16,512]{3,2,1,0:T(8,128)(2,1)S(1)}, u32[]{:S(2)}, u32[]{:S(2)}) collective-permute-start(bf16[1,16,16,512]{3,2,1,0:T(8,128)(2,1)S(1)} %get-tuple-element.378), channel_id=1, source_target_pairs={{0,1},{1,2},{2,3},{3,4},{4,5},{5,6},{6,7},{7,8},{8,9},{9,10},{10,1... | collective-permute-start | bytes 786440 | tf_op jit(solution)/shard_map/while/body/eval_jaxpr/ppermute | solution.py:27
  293.9 13.4 %collective-permute-start.5 = (bf16[1,16,16,512]{3,2,1,0:T(8,128)(2,1)S(1)}, bf16[1,16,16,512]{3,2,1,0:T(8,128)(2,1)S(1)}, u32[]{:S(2)}, u32[]{:S(2)}) collective-permute-start(bf16[1,16,16,512]{3,2,1,0:T(8,128)(2,1)S(1)} %get-tuple-element.378), channel_id=1, source_target_pairs={{1,0},{2,1},{3,2},{4,3},{5,4},{6,5},{7,6},{8,7},{9,8},{10,9},{11,1... | collective-permute-start | bytes 786440 | tf_op jit(solution)/shard_map/while/body/eval_jaxpr/ppermute | solution.py:29
  315.6 8.6 collective-permute-start
  325.2 8.7 collective-permute-start.1
  355.3 10.8 %collective-permute-start.4 = (bf16[1,16,16,512]{3,2,1,0:T(8,128)(2,1)S(1)}, bf16[1,16,16,512]{3,2,1,0:T(8,128)(2,1)S(1)}, u32[]{:S(2)}, u32[]{:S(2)}) collective-permute-start(bf16[1,16,16,512]{3,2,1,0:T(8,128)(2,1)S(1)} %get-tuple-element.378), channel_id=1, source_target_pairs={{0,1},{1,2},{2,3},{3,4},{4,5},{5,6},{6,7},{7,8},{8,9},{9,10},{10,1... | collective-permute-start | bytes 786440 | tf_op jit(solution)/shard_map/while/body/eval_jaxpr/ppermute | solution.py:27
  357.3 13.4 %collective-permute-start.5 = (bf16[1,16,16,512]{3,2,1,0:T(8,128)(2,1)S(1)}, bf16[1,16,16,512]{3,2,1,0:T(8,128)(2,1)S(1)}, u32[]{:S(2)}, u32[]{:S(2)}) collective-permute-start(bf16[1,16,16,512]{3,2,1,0:T(8,128)(2,1)S(1)} %get-tuple-element.378), channel_id=1, source_target_pairs={{1,0},{2,1},{3,2},{4,3},{5,4},{6,5},{7,6},{8,7},{9,8},{10,9},{11,1... | collective-permute-start | bytes 786440 | tf_op jit(solution)/shard_map/while/body/eval_jaxpr/ppermute | solution.py:29
  388.3 8.7 collective-permute-start.1
  397.0 8.4 collective-permute-start.2
  419.2 10.8 %collective-permute-start.4 = (bf16[1,16,16,512]{3,2,1,0:T(8,128)(2,1)S(1)}, bf16[1,16,16,512]{3,2,1,0:T(8,128)(2,1)S(1)}, u32[]{:S(2)}, u32[]{:S(2)}) collective-permute-start(bf16[1,16,16,512]{3,2,1,0:T(8,128)(2,1)S(1)} %get-tuple-element.378), channel_id=1, source_target_pairs={{0,1},{1,2},{2,3},{3,4},{4,5},{5,6},{6,7},{7,8},{8,9},{9,10},{10,1... | collective-permute-start | bytes 786440 | tf_op jit(solution)/shard_map/while/body/eval_jaxpr/ppermute | solution.py:27
  421.2 13.3 %collective-permute-start.5 = (bf16[1,16,16,512]{3,2,1,0:T(8,128)(2,1)S(1)}, bf16[1,16,16,512]{3,2,1,0:T(8,128)(2,1)S(1)}, u32[]{:S(2)}, u32[]{:S(2)}) collective-permute-start(bf16[1,16,16,512]{3,2,1,0:T(8,128)(2,1)S(1)} %get-tuple-element.378), channel_id=1, source_target_pairs={{1,0},{2,1},{3,2},{4,3},{5,4},{6,5},{7,6},{8,7},{9,8},{10,9},{11,1... | collective-permute-start | bytes 786440 | tf_op jit(solution)/shard_map/while/body/eval_jaxpr/ppermute | solution.py:29
  449.3 9.2 collective-permute-start.1
  458.5 9.2 collective-permute-start.2
  476.5 10.7 %collective-permute-start.4 = (bf16[1,16,16,512]{3,2,1,0:T(8,128)(2,1)S(1)}, bf16[1,16,16,512]{3,2,1,0:T(8,128)(2,1)S(1)}, u32[]{:S(2)}, u32[]{:S(2)}) collective-permute-start(bf16[1,16,16,512]{3,2,1,0:T(8,128)(2,1)S(1)} %get-tuple-element.378), channel_id=1, source_target_pairs={{0,1},{1,2},{2,3},{3,4},{4,5},{5,6},{6,7},{7,8},{8,9},{9,10},{10,1... | collective-permute-start | bytes 786440 | tf_op jit(solution)/shard_map/while/body/eval_jaxpr/ppermute | solution.py:27
  478.5 10.6 %collective-permute-start.5 = (bf16[1,16,16,512]{3,2,1,0:T(8,128)(2,1)S(1)}, bf16[1,16,16,512]{3,2,1,0:T(8,128)(2,1)S(1)}, u32[]{:S(2)}, u32[]{:S(2)}) collective-permute-start(bf16[1,16,16,512]{3,2,1,0:T(8,128)(2,1)S(1)} %get-tuple-element.378), channel_id=1, source_target_pairs={{1,0},{2,1},{3,2},{4,3},{5,4},{6,5},{7,6},{8,7},{9,8},{10,9},{11,1... | collective-permute-start | bytes 786440 | tf_op jit(solution)/shard_map/while/body/eval_jaxpr/ppermute | solution.py:29
  491.1 18.7 %collective-permute-start = (bf16[1,16,16,512]{3,2,1,0:T(8,128)(2,1)}, bf16[1,16,16,512]{3,2,1,0:T(8,128)(2,1)S(1)}, u32[]{:S(2)}, u32[]{:S(2)}) collective-permute-start(bf16[1,16,16,512]{3,2,1,0:T(8,128)(2,1)} %get-tuple-element.343), channel_id=1, source_target_pairs={{0,32},{32,64},{64,96},{96,128},{128,160},{160,192},{192,224},{1,3... | collective-permute-start | bytes 786440 | tf_op jit(solution)/shard_map/while/body/eval_jaxpr/ppermute | solution.py:12
  510.8 11.3 %collective-permute-start.1 = (bf16[1,16,16,512]{3,2,1,0:T(8,128)(2,1)S(1)}, bf16[1,16,16,512]{3,2,1,0:T(8,128)(2,1)S(1)}, u32[]{:S(2)}, u32[]{:S(2)}) collective-permute-start(bf16[1,16,16,512]{3,2,1,0:T(8,128)(2,1)S(1)} %bitcast_select_fusion.2), channel_id=1, source_target_pairs={{0,32},{32,0},{64,96},{96,64},{128,160},{160,128},{192,224},{224,1... | collective-permute-start | bytes 786440 | tf_op jit(solution)/shard_map/while/body/eval_jaxpr/ppermute | solution.py:16
  538.7 10.8 %collective-permute-start.4 = (bf16[1,16,16,512]{3,2,1,0:T(8,128)(2,1)S(1)}, bf16[1,16,16,512]{3,2,1,0:T(8,128)(2,1)S(1)}, u32[]{:S(2)}, u32[]{:S(2)}) collective-permute-start(bf16[1,16,16,512]{3,2,1,0:T(8,128)(2,1)S(1)} %get-tuple-element.378), channel_id=1, source_target_pairs={{0,1},{1,2},{2,3},{3,4},{4,5},{5,6},{6,7},{7,8},{8,9},{9,10},{10,1... | collective-permute-start | bytes 786440 | tf_op jit(solution)/shard_map/while/body/eval_jaxpr/ppermute | solution.py:27
  540.6 13.0 %collective-permute-start.5 = (bf16[1,16,16,512]{3,2,1,0:T(8,128)(2,1)S(1)}, bf16[1,16,16,512]{3,2,1,0:T(8,128)(2,1)S(1)}, u32[]{:S(2)}, u32[]{:S(2)}) collective-permute-start(bf16[1,16,16,512]{3,2,1,0:T(8,128)(2,1)S(1)} %get-tuple-element.378), channel_id=1, source_target_pairs={{1,0},{2,1},{3,2},{4,3},{5,4},{6,5},{7,6},{8,7},{9,8},{10,9},{11,1... | collective-permute-start | bytes 786440 | tf_op jit(solution)/shard_map/while/body/eval_jaxpr/ppermute | solution.py:29
  562.9 21.5 %collective-permute-start.1 = (bf16[1,16,16,512]{3,2,1,0:T(8,128)(2,1)S(1)}, bf16[1,16,16,512]{3,2,1,0:T(8,128)(2,1)S(1)}, u32[]{:S(2)}, u32[]{:S(2)}) collective-permute-start(bf16[1,16,16,512]{3,2,1,0:T(8,128)(2,1)S(1)} %bitcast_select_fusion.2), channel_id=1, source_target_pairs={{0,32},{32,0},{64,96},{96,64},{128,160},{160,128},{192,224},{224,1... | collective-permute-start | bytes 786440 | tf_op jit(solution)/shard_map/while/body/eval_jaxpr/ppermute | solution.py:16
  584.3 9.0 collective-permute-start.2
  601.8 10.8 %collective-permute-start.4 = (bf16[1,16,16,512]{3,2,1,0:T(8,128)(2,1)S(1)}, bf16[1,16,16,512]{3,2,1,0:T(8,128)(2,1)S(1)}, u32[]{:S(2)}, u32[]{:S(2)}) collective-permute-start(bf16[1,16,16,512]{3,2,1,0:T(8,128)(2,1)S(1)} %get-tuple-element.378), channel_id=1, source_target_pairs={{0,1},{1,2},{2,3},{3,4},{4,5},{5,6},{6,7},{7,8},{8,9},{9,10},{10,1... | collective-permute-start | bytes 786440 | tf_op jit(solution)/shard_map/while/body/eval_jaxpr/ppermute | solution.py:27
  603.8 12.2 %collective-permute-start.5 = (bf16[1,16,16,512]{3,2,1,0:T(8,128)(2,1)S(1)}, bf16[1,16,16,512]{3,2,1,0:T(8,128)(2,1)S(1)}, u32[]{:S(2)}, u32[]{:S(2)}) collective-permute-start(bf16[1,16,16,512]{3,2,1,0:T(8,128)(2,1)S(1)} %get-tuple-element.378), channel_id=1, source_target_pairs={{1,0},{2,1},{3,2},{4,3},{5,4},{6,5},{7,6},{8,7},{9,8},{10,9},{11,1... | collective-permute-start | bytes 786440 | tf_op jit(solution)/shard_map/while/body/eval_jaxpr/ppermute | solution.py:29
  618.0 10.4 %collective-permute-start = (bf16[1,16,16,512]{3,2,1,0:T(8,128)(2,1)}, bf16[1,16,16,512]{3,2,1,0:T(8,128)(2,1)S(1)}, u32[]{:S(2)}, u32[]{:S(2)}) collective-permute-start(bf16[1,16,16,512]{3,2,1,0:T(8,128)(2,1)} %get-tuple-element.343), channel_id=1, source_target_pairs={{0,32},{32,64},{64,96},{96,128},{128,160},{160,192},{192,224},{1,3... | collective-permute-start | bytes 786440 | tf_op jit(solution)/shard_map/while/body/eval_jaxpr/ppermute | solution.py:12
  629.4 8.5 collective-permute-start.1
  637.9 16.8 %collective-permute-start.2 = (bf16[1,16,16,512]{3,2,1,0:T(8,128)(2,1)S(1)}, bf16[1,16,16,512]{3,2,1,0:T(8,128)(2,1)S(1)}, u32[]{:S(2)}, u32[]{:S(2)}) collective-permute-start(bf16[1,16,16,512]{3,2,1,0:T(8,128)(2,1)S(1)} %collective-permute-done.1), channel_id=1, source_target_pairs={{0,64},{32,96},{64,0},{96,32},{128,192},{160,224},{192,128},{224,1... | collective-permute-start | bytes 786440 | tf_op jit(solution)/shard_map/while/body/eval_jaxpr/ppermute | solution.py:16
  654.7 9.6 collective-permute-start.3
  664.9 10.8 %collective-permute-start.4 = (bf16[1,16,16,512]{3,2,1,0:T(8,128)(2,1)S(1)}, bf16[1,16,16,512]{3,2,1,0:T(8,128)(2,1)S(1)}, u32[]{:S(2)}, u32[]{:S(2)}) collective-permute-start(bf16[1,16,16,512]{3,2,1,0:T(8,128)(2,1)S(1)} %get-tuple-element.378), channel_id=1, source_target_pairs={{0,1},{1,2},{2,3},{3,4},{4,5},{5,6},{6,7},{7,8},{8,9},{9,10},{10,1... | collective-permute-start | bytes 786440 | tf_op jit(solution)/shard_map/while/body/eval_jaxpr/ppermute | solution.py:27
  666.8 10.7 %collective-permute-start.5 = (bf16[1,16,16,512]{3,2,1,0:T(8,128)(2,1)S(1)}, bf16[1,16,16,512]{3,2,1,0:T(8,128)(2,1)S(1)}, u32[]{:S(2)}, u32[]{:S(2)}) collective-permute-start(bf16[1,16,16,512]{3,2,1,0:T(8,128)(2,1)S(1)} %get-tuple-element.378), channel_id=1, source_target_pairs={{1,0},{2,1},{3,2},{4,3},{5,4},{6,5},{7,6},{8,7},{9,8},{10,9},{11,1... | collective-permute-start | bytes 786440 | tf_op jit(solution)/shard_map/while/body/eval_jaxpr/ppermute | solution.py:29
  679.6 10.7 %collective-permute-start = (bf16[1,16,16,512]{3,2,1,0:T(8,128)(2,1)}, bf16[1,16,16,512]{3,2,1,0:T(8,128)(2,1)S(1)}, u32[]{:S(2)}, u32[]{:S(2)}) collective-permute-start(bf16[1,16,16,512]{3,2,1,0:T(8,128)(2,1)} %get-tuple-element.343), channel_id=1, source_target_pairs={{0,32},{32,64},{64,96},{96,128},{128,160},{160,192},{192,224},{1,3... | collective-permute-start | bytes 786440 | tf_op jit(solution)/shard_map/while/body/eval_jaxpr/ppermute | solution.py:12
  699.2 17.3 %collective-permute-start.2 = (bf16[1,16,16,512]{3,2,1,0:T(8,128)(2,1)S(1)}, bf16[1,16,16,512]{3,2,1,0:T(8,128)(2,1)S(1)}, u32[]{:S(2)}, u32[]{:S(2)}) collective-permute-start(bf16[1,16,16,512]{3,2,1,0:T(8,128)(2,1)S(1)} %collective-permute-done.1), channel_id=1, source_target_pairs={{0,64},{32,96},{64,0},{96,32},{128,192},{160,224},{192,128},{224,1... | collective-permute-start | bytes 786440 | tf_op jit(solution)/shard_map/while/body/eval_jaxpr/ppermute | solution.py:16
  716.5 10.5 %collective-permute-start.3 = (bf16[1,16,16,512]{3,2,1,0:T(8,128)(2,1)S(1)}, bf16[1,16,16,512]{3,2,1,0:T(8,128)(2,1)S(1)}, u32[]{:S(2)}, u32[]{:S(2)}) collective-permute-start(bf16[1,16,16,512]{3,2,1,0:T(8,128)(2,1)S(1)} %collective-permute-done.2), channel_id=1, source_target_pairs={{0,128},{32,160},{64,192},{96,224},{128,0},{160,32},{192,64},{224,... | collective-permute-start | bytes 786440 | tf_op jit(solution)/shard_map/while/body/eval_jaxpr/ppermute | solution.py:16
  727.6 10.8 %collective-permute-start.4 = (bf16[1,16,16,512]{3,2,1,0:T(8,128)(2,1)S(1)}, bf16[1,16,16,512]{3,2,1,0:T(8,128)(2,1)S(1)}, u32[]{:S(2)}, u32[]{:S(2)}) collective-permute-start(bf16[1,16,16,512]{3,2,1,0:T(8,128)(2,1)S(1)} %get-tuple-element.378), channel_id=1, source_target_pairs={{0,1},{1,2},{2,3},{3,4},{4,5},{5,6},{6,7},{7,8},{8,9},{9,10},{10,1... | collective-permute-start | bytes 786440 | tf_op jit(solution)/shard_map/while/body/eval_jaxpr/ppermute | solution.py:27
  729.6 13.1 %collective-permute-start.5 = (bf16[1,16,16,512]{3,2,1,0:T(8,128)(2,1)S(1)}, bf16[1,16,16,512]{3,2,1,0:T(8,128)(2,1)S(1)}, u32[]{:S(2)}, u32[]{:S(2)}) collective-permute-start(bf16[1,16,16,512]{3,2,1,0:T(8,128)(2,1)S(1)} %get-tuple-element.378), channel_id=1, source_target_pairs={{1,0},{2,1},{3,2},{4,3},{5,4},{6,5},{7,6},{8,7},{9,8},{10,9},{11,1... | collective-permute-start | bytes 786440 | tf_op jit(solution)/shard_map/while/body/eval_jaxpr/ppermute | solution.py:29
  767.6 23.5 %collective-permute-start.3 = (bf16[1,16,16,512]{3,2,1,0:T(8,128)(2,1)S(1)}, bf16[1,16,16,512]{3,2,1,0:T(8,128)(2,1)S(1)}, u32[]{:S(2)}, u32[]{:S(2)}) collective-permute-start(bf16[1,16,16,512]{3,2,1,0:T(8,128)(2,1)S(1)} %collective-permute-done.2), channel_id=1, source_target_pairs={{0,128},{32,160},{64,192},{96,224},{128,0},{160,32},{192,64},{224,... | collective-permute-start | bytes 786440 | tf_op jit(solution)/shard_map/while/body/eval_jaxpr/ppermute | solution.py:16
  791.7 10.8 %collective-permute-start.4 = (bf16[1,16,16,512]{3,2,1,0:T(8,128)(2,1)S(1)}, bf16[1,16,16,512]{3,2,1,0:T(8,128)(2,1)S(1)}, u32[]{:S(2)}, u32[]{:S(2)}) collective-permute-start(bf16[1,16,16,512]{3,2,1,0:T(8,128)(2,1)S(1)} %get-tuple-element.378), channel_id=1, source_target_pairs={{0,1},{1,2},{2,3},{3,4},{4,5},{5,6},{6,7},{7,8},{8,9},{9,10},{10,1... | collective-permute-start | bytes 786440 | tf_op jit(solution)/shard_map/while/body/eval_jaxpr/ppermute | solution.py:27
  793.6 13.3 %collective-permute-start.5 = (bf16[1,16,16,512]{3,2,1,0:T(8,128)(2,1)S(1)}, bf16[1,16,16,512]{3,2,1,0:T(8,128)(2,1)S(1)}, u32[]{:S(2)}, u32[]{:S(2)}) collective-permute-start(bf16[1,16,16,512]{3,2,1,0:T(8,128)(2,1)S(1)} %get-tuple-element.378), channel_id=1, source_target_pairs={{1,0},{2,1},{3,2},{4,3},{5,4},{6,5},{7,6},{8,7},{9,8},{10,9},{11,1... | collective-permute-start | bytes 786440 | tf_op jit(solution)/shard_map/while/body/eval_jaxpr/ppermute | solution.py:29
  826.7 9.2 collective-permute-start.2
  835.9 20.8 %collective-permute-start.3 = (bf16[1,16,16,512]{3,2,1,0:T(8,128)(2,1)S(1)}, bf16[1,16,16,512]{3,2,1,0:T(8,128)(2,1)S(1)}, u32[]{:S(2)}, u32[]{:S(2)}) collective-permute-start(bf16[1,16,16,512]{3,2,1,0:T(8,128)(2,1)S(1)} %collective-permute-done.2), channel_id=1, source_target_pairs={{0,128},{32,160},{64,192},{96,224},{128,0},{160,32},{192,64},{224,... | collective-permute-start | bytes 786440 | tf_op jit(solution)/shard_map/while/body/eval_jaxpr/ppermute | solution.py:16
  857.3 10.8 %collective-permute-start.4 = (bf16[1,16,16,512]{3,2,1,0:T(8,128)(2,1)S(1)}, bf16[1,16,16,512]{3,2,1,0:T(8,128)(2,1)S(1)}, u32[]{:S(2)}, u32[]{:S(2)}) collective-permute-start(bf16[1,16,16,512]{3,2,1,0:T(8,128)(2,1)S(1)} %get-tuple-element.378), channel_id=1, source_target_pairs={{0,1},{1,2},{2,3},{3,4},{4,5},{5,6},{6,7},{7,8},{8,9},{9,10},{10,1... | collective-permute-start | bytes 786440 | tf_op jit(solution)/shard_map/while/body/eval_jaxpr/ppermute | solution.py:27
  859.2 13.3 %collective-permute-start.5 = (bf16[1,16,16,512]{3,2,1,0:T(8,128)(2,1)S(1)}, bf16[1,16,16,512]{3,2,1,0:T(8,128)(2,1)S(1)}, u32[]{:S(2)}, u32[]{:S(2)}) collective-permute-start(bf16[1,16,16,512]{3,2,1,0:T(8,128)(2,1)S(1)} %get-tuple-element.378), channel_id=1, source_target_pairs={{1,0},{2,1},{3,2},{4,3},{5,4},{6,5},{7,6},{8,7},{9,8},{10,9},{11,1... | collective-permute-start | bytes 786440 | tf_op jit(solution)/shard_map/while/body/eval_jaxpr/ppermute | solution.py:29
  (34 other events, 200.6 us)
Sparse Core Ops, SparseCore 0:
  10.0 55.0 all-gather.7
  67.7 60.6 all-gather.3
  131.1 60.4 all-gather.5
  875.8 91.8 all-reduce.3
where the time goes:
time: 978 us; the launch traced here: 976 us
  waiting for transfers between devices  577 us (59%)
  starting transfers between devices  273 us (28%)
  matrix products  46.2 us (5%)
  other arithmetic  32.5 us (3%)
  loops' own time  17.3 us (2%)
  local copies, waits for them, and re-layouts  17 us (2%)
  between operations  13.2 us (1%)
    ppermute x33, waiting for transfers between devices, partner(): lax.ppermute(shard, axis, [(i, i ^ 1 << bit) for i in range(lax.axis_size...  190 us
    ppermute x33, starting transfers between devices, partner(): lax.ppermute(shard, axis, [(i, i ^ 1 << bit) for i in range(lax.axis_size...  141 us
    psum x1, waiting for transfers between devices, broadcast(): return lax.psum(jnp.where(mine, shard, jnp.zeros_like(shard)), axis)  92 us
    ppermute x11, starting transfers between devices, extended_2(): lax.ppermute(head, axis, [((i + 1) % count, i) for i in range(ends)])  73.2 us
    all_gather x1, waiting for transfers between devices, on_device(): lax.all_gather(conv_first, 'frame', axis=2, tiled=True)  63.4 us
    all_gather x1, waiting for transfers between devices, on_device(): lax.all_gather(conv_second, 'frame', axis=2, tiled=True)  63.1 us
    all_gather x1, waiting for transfers between devices, on_device(): lax.all_gather(temporal, 'frame', axis=2, tiled=True)  56.3 us
    ppermute x11, waiting for transfers between devices, passed_along(): return lax.ppermute(shard, axis, pairs)  47.2 us
  transfers between devices with their start and end apart: 70, of which 70 were waited for; matrix products, arithmetic and copies ran while one was open for 1% of the time, Pallas kernels for 0%

commit v1 on v0

v1 whole, which is shorter than its diff:
```python
import itertools

import jax
import jax.numpy as jnp
from jax import lax
from jax.experimental import pallas as pl
from jax.experimental.pallas import tpu as pltpu
from jax.sharding import Mesh
from jax.sharding import PartitionSpec as P

skip_scale = 0.7071067811865476
AXES = ("y", "zlo", "x", "zhi", "core")
SEGMENT = ("y", "zlo")
FRAME = ("x", "zhi", "core")
PLANE = ("zlo", "x", "zhi", "core")
NY, NX, NZ = 4, 4, 8
SIDE = 16
CH = 512
PIX = SIDE * SIDE
F32 = jnp.float32
BF16 = jnp.bfloat16


def flat(x, y, z, core):
    return (((y * 2 + z % 2) * 4 + x) * 4 + z // 2) * 2 + core


def sent(value, route):
    pairs = []
    for x, y, z, core in itertools.product(range(NX), range(NY), range(NZ), range(2)):
        target = route(x, y, z, core)
        if target is not None:
            pairs.append((flat(x, y, z, core), flat(*target)))
    return lax.ppermute(value, AXES, pairs)


def to_right(x, y, z, core):
    q = 2 * z + core + 1
    return (x, y, q // 2, q % 2) if q < 2 * NZ else None


def to_left(x, y, z, core):
    q = 2 * z + core - 1
    return (x, y, q // 2, q % 2) if q >= 0 else None


def plane_to_plane(source, target):
    return lambda x, y, z, core: (x, target, z, core) if y == source else None


def silu(u):
    return u / (1.0 + jnp.exp(-u))


def widen(frame, wide_ref, index):
    full = frame.astype(F32)
    column = lax.broadcasted_iota(jnp.int32, (PIX, CH), 0) % SIDE
    before = jnp.where(column == 0, 0.0, pltpu.roll(full, 1, 0)).astype(BF16)
    after = jnp.where(column == SIDE - 1, 0.0, pltpu.roll(full, PIX - 1, 0)).astype(BF16)
    edge = jnp.zeros((SIDE, 3 * CH), BF16)
    wide_ref[index, 0:SIDE, :] = edge
    wide_ref[index, SIDE + PIX : 2 * SIDE + PIX, :] = edge
    wide_ref[index, SIDE : SIDE + PIX, 0:CH] = before
    wide_ref[index, SIDE : SIDE + PIX, CH : 2 * CH] = frame
    wide_ref[index, SIDE : SIDE + PIX, 2 * CH : 3 * CH] = after


def conv_rows(wide_ref, weights, index, dy):
    rows = wide_ref[index, pl.ds(pl.multiple_of(dy * SIDE, SIDE), PIX), :]
    return jnp.dot(rows, weights, preferred_element_type=F32)


def first_kernel(e_ref, w_ref, out_ref, wide_ref, acc_ref):
    dy = pl.program_id(0)
    frames = e_ref.shape[0]

    @pl.when(dy == 0)
    def _():
        for i in range(frames):
            widen(e_ref[i], wide_ref, i)

    weights = w_ref[...].reshape(3 * CH, CH)
    for i in range(frames):
        part = conv_rows(wide_ref, weights, i, dy)

        @pl.when(dy == 0)
        def _():
            acc_ref[i] = part

        @pl.when(dy == 1)
        def _():
            acc_ref[i] += part

        @pl.when(dy == 2)
        def _():
            out_ref[i] = silu(acc_ref[i] + part).astype(BF16)


def second_kernel(a_ref, w_ref, acc_ref, wide_ref):
    step = pl.program_id(0)
    frames = a_ref.shape[0]

    @pl.when(step == 0)
    def _():
        for i in range(frames):
            widen(a_ref[i], wide_ref, i)

    @pl.when(step < 3)
    def _():
        weights = w_ref[...].reshape(3 * CH, CH)
        for i in range(frames):
            part = conv_rows(wide_ref, weights, i, step)

            @pl.when(step == 0)
            def _():
                acc_ref[i] = part

            @pl.when(step > 0)
            def _():
                acc_ref[i] += part

    @pl.when(step == 3)
    def _():
        for i in range(frames):
            total = acc_ref[i]
            for j in range(max(0, i - 1), min(frames, i + 2)):
                total += jnp.dot(a_ref[j], w_ref[j - i + 1], preferred_element_type=F32)
            acc_ref[i] = total


def last_kernel(acc_ref, e_ref, left_ref, right_ref, w_ref, out_ref):
    last = e_ref.shape[0] - 1
    for i in range(last + 1):
        total = acc_ref[i]
        if i == 0:
            total += jnp.dot(left_ref[...], w_ref[0], preferred_element_type=F32)
        if i == last:
            total += jnp.dot(right_ref[...], w_ref[2], preferred_element_type=F32)
        out_ref[i] = (e_ref[i].astype(F32) + silu(total)).astype(BF16)


def whole(*shape):
    return pl.BlockSpec(shape, lambda *_: (0,) * len(shape))


def params(mib):
    return pltpu.CompilerParams(vmem_limit_bytes=mib << 20)


def cost(taps, weight_taps):
    return pl.CostEstimate(
        flops=2 * taps * PIX * CH * CH,
        bytes_accessed=weight_taps * CH * CH * 2 + 4 * PIX * CH * 2,
        transcendentals=2 * PIX * CH,
    )


def section(e, first, second, which):
    frames = e.shape[0]
    activated = pl.pallas_call(
        first_kernel,
        grid=(3,),
        in_specs=[
            whole(frames, PIX, CH),
            pl.BlockSpec((3, CH, CH), lambda i: (i, which, 0)),
        ],
        out_specs=whole(frames, PIX, CH),
        out_shape=jax.ShapeDtypeStruct((frames, PIX, CH), BF16),
        scratch_shapes=[
            pltpu.VMEM((frames, PIX + 2 * SIDE, 3 * CH), BF16),
            pltpu.VMEM((frames, PIX, CH), F32),
        ],
        compiler_params=params(20),
        cost_estimate=cost(9 * frames, 9),
        name="conv_first",
    )(e, first)
    left = sent(activated[frames - 1], to_right)
    right = sent(activated[0], to_left)
    acc = pl.pallas_call(
        second_kernel,
        grid=(4,),
        in_specs=[
            whole(frames, PIX, CH),
            pl.BlockSpec((3, CH, CH), lambda i: (i, which, 0)),
        ],
        out_specs=whole(frames, PIX, CH),
        out_shape=jax.ShapeDtypeStruct((frames, PIX, CH), F32),
        scratch_shapes=[pltpu.VMEM((frames, PIX + 2 * SIDE, 3 * CH), BF16)],
        compiler_params=params(20),
        cost_estimate=cost(11 * frames, 12),
        name="conv_second",
    )(activated, second)
    return pl.pallas_call(
        last_kernel,
        grid=(1,),
        in_specs=[
            whole(frames, PIX, CH),
            whole(frames, PIX, CH),
            whole(PIX, CH),
            whole(PIX, CH),
            pl.BlockSpec((3, CH, CH), lambda i: (3, which, 0)),
        ],
        out_specs=whole(frames, PIX, CH),
        out_shape=jax.ShapeDtypeStruct((frames, PIX, CH), BF16),
        compiler_params=params(20),
        cost_estimate=cost(2, 3),
        name="halo_and_residual",
    )(acc, e, left, right, second)


def joined(h, skip):
    return ((h.astype(F32) + skip.astype(F32)) * skip_scale).astype(BF16)


def spread_clips(noisy):
    zlo, core, x = lax.axis_index("zlo"), lax.axis_index("core"), lax.axis_index("x")
    clips = noisy.reshape(4, PIX, CH)
    got = []
    for r in range(2):
        clip = lax.dynamic_index_in_dim(clips, 2 * zlo + (r ^ core), 0, keepdims=False)

        def route(sx, sy, sz, sc, r=r):
            hi, lo = sz // 2, sz % 2
            return (2 * lo + (r ^ sc), sy, 2 * sx + hi // 2, hi % 2)

        got.append(sent(clip, route))
    even = x % 2 == 0
    return jnp.stack([jnp.where(even, got[0], got[1]), jnp.where(even, got[1], got[0])])


def deliver(h):
    y, zlo, core, x = (lax.axis_index(n) for n in ("y", "zlo", "core", "x"))
    rows = h.reshape(2, NY, 2, 2, SIDE, CH)
    mine = rows[:, NY - 1]
    for target in range(NY - 1):
        got = sent(rows[:, target], plane_to_plane(NY - 1, target))
        mine = jnp.where(y == target, got, mine)
    messages = mine.reshape(4, 2, SIDE, CH)
    slots = []
    for r in range(4):
        message = lax.dynamic_index_in_dim(messages, x ^ r, 0, keepdims=False)

        def route(sx, sy, sz, sc, r=r):
            k, lo = (sx ^ r) // 2, (sx ^ r) % 2
            return (sz // 2, sy, 2 * (2 * (sz % 2) + sc) + lo, k)

        slots.append(sent(message, route))
    slots = jnp.stack(slots)
    here = core * 2 + zlo
    out = [lax.dynamic_index_in_dim(slots, here ^ c, 0, keepdims=False) for c in range(4)]
    return jnp.stack(out)[:, None]


def on_device(noisy, conv_first, conv_second, temporal):
    first = lax.all_gather(conv_first[0], PLANE, axis=1, tiled=True)
    tail = jnp.concatenate([conv_second[0], temporal[0]], axis=0)
    second = lax.all_gather(tail, PLANE, axis=1, tiled=True)
    e0 = spread_clips(noisy)
    e1 = section(e0, first, second, 0)
    skip6 = sent(e1, plane_to_plane(0, 3))
    h = section(e1, first, second, 1)
    e2 = sent(h, plane_to_plane(0, 1))
    skip5 = sent(e2, plane_to_plane(1, 2))
    e3 = section(e2, first, second, 0)
    h = section(e3, first, second, 1)
    e4 = sent(joined(h, e3), plane_to_plane(1, 2))
    h = section(e4, first, second, 0)
    h = section(joined(h, skip5), first, second, 1)
    h = sent(h, plane_to_plane(2, 3))
    h = section(joined(h, skip6), first, second, 0)
    h = section(joined(h, e0), first, second, 1)
    return deliver(h)


def solution(mesh):
    fine = Mesh(mesh.devices.reshape(NY, 2, NX, NZ // 2, 2), AXES)
    weight_spec = P(SEGMENT, None, FRAME, None)
    return jax.shard_map(
        on_device,
        mesh=fine,
        in_specs=(P(None, FRAME), weight_spec, weight_spec, weight_spec),
        out_specs=P(None, FRAME, SEGMENT),
        check_vma=False,
    )
```

time: 978 us -> 499 us (0.51)
  waiting for transfers between devices: 577 us -> 313 us
  starting transfers between devices: 273 us -> 75.3 us
  Pallas kernels: 0 us -> 82.4 us
  matrix products: 46.2 us -> 0 us
  other arithmetic: 32.5 us -> 3.08 us
  loops' own time: 17.3 us -> 0 us
    ppermute x66 -> x30, waiting for transfers between devices: 300 us -> 62 us  [sent(): return lax.ppermute(value, AXES, pairs)]
    ppermute x66 -> x30, starting transfers between devices: 273 us -> 75.3 us  [sent(): return lax.ppermute(value, AXES, pairs)]
    psum x1 -> x0, waiting for transfers between devices: 92 us -> none  [broadcast(): return lax.psum(jnp.where(mine, shard, jnp.zeros_like(shard)), axis)]
    pallas_call x0 -> x24, Pallas kernels: none -> 82.4 us  [the longest x8 41.4 us: section(): pl.pallas_call(second_kernel, grid=(4,), in_specs=[whole(frames, PIX, CH)...]
    all_gather x3 -> x2, waiting for transfers between devices: 183 us -> 251 us  [the longest x1 137 us: on_device(): first = lax.all_gather(conv_first[0], PLANE, axis=1, tiled=True)]
    dot_general x84 -> x0, matrix products: 46.2 us -> none  [the longest x72 39.4 us: spatial(): jnp.dot(window, kernel[3 * row_shift + col_shift], preferred_element_type...]
    select_n x45 -> x1, other arithmetic: 31.7 us -> 0.03 us  [deliver(): mine = jnp.where(y == target, got, mine)]
    another operation x23 -> x0, loops' own time: 17.3 us -> none  [the longest x1 16.3 us: on_device(): lax.scan(tick_step, (prev_out, side_store, out_store), jnp.arange(tick_co...]
  transfers between devices with their start and end apart: 70 -> 32, of which waited for: 70 -> 7; matrix products, arithmetic and copies ran while one was open for 1% -> 1% of each run, Pallas kernels for 0% -> 11%
where the time goes in v1:
time: 499 us; the launch traced here: 498 us
  waiting for transfers between devices  313 us (63%)
  Pallas kernels  82.4 us (17%)
  starting transfers between devices  75.3 us (15%)
  between operations  14.3 us (3%)
  local copies, waits for them, and re-layouts  9.7 us (2%)
    all_gather x1, waiting for transfers between devices, on_device(): first = lax.all_gather(conv_first[0], PLANE, axis=1, tiled=True)  137 us
    all_gather x1, waiting for transfers between devices, on_device(): second = lax.all_gather(tail, PLANE, axis=1, tiled=True)  113 us
    ppermute x30, starting transfers between devices, sent(): return lax.ppermute(value, AXES, pairs)  75.3 us
    ppermute x30, waiting for transfers between devices, sent(): return lax.ppermute(value, AXES, pairs)  62 us
    pallas_call x8, Pallas kernels, section(): pl.pallas_call(second_kernel, grid=(4,), in_specs=[whole(frames, PIX, CH)...  41.4 us
    pallas_call x8, Pallas kernels, section(): pl.pallas_call(first_kernel, grid=(3,), in_specs=[whole(frames, PIX, CH),...  36.4 us
  transfers between devices with their start and end apart: 32, of which 7 were waited for; matrix products, arithmetic and copies ran while one was open for 1% of the time, Pallas kernels for 11%

profile of v1, /device:TPU:2, one launch (start us, length us, event | category | flops | bytes accessed | tf_op | source)
XLA Modules:
  0.0 498.0 jit_solution(8447206877007640596)
XLA Ops:
  7.3 1.6 pad_maximum_fusion.1
  10.0 5.2 %collective-permute-start = (bf16[256,512]{1,0:T(8,128)(2,1)S(1)}, bf16[256,512]{1,0:T(8,128)(2,1)S(1)}, u32[]{:S(2)}, u32[]{:S(2)}) collective-permute-start(bf16[256,512]{1,0:T(8,128)(2,1)S(1)} %get-tuple-element.5), channel_id=1, source_target_pairs={{0,0},{1,8},{32,16},{33,24},{2,1},{3,9},{34,17},{35,25},{4,32},{5,... | collective-permute-start | bytes 786440 | tf_op jit(solution)/shard_map/ppermute | solution.py:34
  15.3 6.5 %collective-permute-done = bf16[256,512]{1,0:T(8,128)(2,1)S(1)} collective-permute-done((bf16[256,512]{1,0:T(8,128)(2,1)S(1)}, bf16[256,512]{1,0:T(8,128)(2,1)S(1)}, u32[]{:S(2)}, u32[]{:S(2)}) %collective-permute-start) | collective-permute-done | bytes 262176 | tf_op jit(solution)/shard_map/ppermute | solution.py:34
  21.9 5.2 %collective-permute-done.1 = bf16[256,512]{1,0:T(8,128)(2,1)S(1)} collective-permute-done((bf16[256,512]{1,0:T(8,128)(2,1)S(1)}, bf16[256,512]{1,0:T(8,128)(2,1)S(1)}, u32[]{:S(2)}, u32[]{:S(2)}) %collective-permute-start.1) | collective-permute-done | bytes 262176 | tf_op jit(solution)/shard_map/ppermute | solution.py:34
  27.2 137.1 %all-gather.6.cloned.1.call-done = bf16[1,9,1024,512]{3,2,1,0:T(8,128)(2,1)} async-done(((bf16[1,9,16,512]{3,2,1,0:T(8,128)(2,1)}), bf16[1,9,1024,512]{3,2,1,0:T(8,128)(2,1)}) %all-gather.6.cloned.1.call-update) | async-done | bytes 9437200 | tf_op jit(solution)/shard_map/all_gather | solution.py:255
  164.2 3.7 copy-done.1
  167.9 4.5 conv_first.8.a_ref
  172.5 2.2 collective-permute-start.2
  174.7 1.3 collective-permute-start.3
  176.0 113.4 %all-gather.4.cloned.1.call-done.w_ref = bf16[12,1024,512]{2,1,0:T(8,128)(2,1)} async-done(((bf16[12,16,512]{2,1,0:T(8,128)(2,1)}), bf16[12,1024,512]{2,1,0:T(8,128)(2,1)}) %all-gather.4.cloned.1.call-update) | async-done | bytes 12582928 | tf_op jit(solution)/shard_map/all_gather | solution.py:257
  289.4 4.6 copy-done
  294.0 5.2 %conv_second.8.acc_ref = f32[2,256,512]{2,1,0:T(8,128)S(1)} custom-call(bf16[2,256,512]{2,1,0:T(8,128)(2,1)S(1)} %conv_first.8.a_ref, bf16[12,1024,512]{2,1,0:T(8,128)(2,1)S(1)} %copy-done), custom_call_target="tpu_custom_call" | custom-call | flops 2952790016 | bytes 7340032 | tf_op jit(solution)/shard_map/conv_second/pallas_call | solution.py:179
  299.8 4.5 conv_first.9.a_ref
  304.4 2.2 collective-permute-start.4
  306.6 1.3 collective-permute-start.5
  307.9 5.2 %conv_second.9.acc_ref = f32[2,256,512]{2,1,0:T(8,128)S(1)} custom-call(bf16[2,256,512]{2,1,0:T(8,128)(2,1)S(1)} %conv_first.9.a_ref, bf16[12,1024,512]{2,1,0:T(8,128)(2,1)S(1)} %bitcast.81), custom_call_target="tpu_custom_call" | custom-call | flops 2952790016 | bytes 7340032 | tf_op jit(solution)/shard_map/conv_second/pallas_call | solution.py:179
  313.7 3.1 collective-permute-start.6
  316.8 10.1 %collective-permute-done.6.e_ref = bf16[2,256,512]{2,1,0:T(8,128)(2,1)S(1)} collective-permute-done((bf16[2,256,512]{2,1,0:T(8,128)(2,1)S(1)}, bf16[2,256,512]{2,1,0:T(8,128)(2,1)S(1)}, u32[]{:S(2)}, u32[]{:S(2)}) %collective-permute-start.6) | collective-permute-done | bytes 524320 | tf_op jit(solution)/shard_map/ppermute | solution.py:34
  326.9 4.5 conv_first.10.a_ref
  331.5 4.2 collective-permute-start.7
  335.7 1.5 collective-permute-start.8
  337.2 5.2 %conv_second.10.acc_ref = f32[2,256,512]{2,1,0:T(8,128)S(1)} custom-call(bf16[2,256,512]{2,1,0:T(8,128)(2,1)S(1)} %conv_first.10.a_ref, bf16[12,1024,512]{2,1,0:T(8,128)(2,1)S(1)} %bitcast.81), custom_call_target="tpu_custom_call" | custom-call | flops 2952790016 | bytes 7340032 | tf_op jit(solution)/shard_map/conv_second/pallas_call | solution.py:179
  343.0 4.5 conv_first.11.a_ref
  347.6 1.3 collective-permute-start.10
  348.9 6.7 %collective-permute-start.9 = (bf16[256,512]{1,0:T(8,128)(2,1)S(1)}, bf16[256,512]{1,0:T(8,128)(2,1)S(1)}, u32[]{:S(2)}, u32[]{:S(2)}) collective-permute-start(bf16[256,512]{1,0:T(8,128)(2,1)S(1)} %get-tuple-element.19), channel_id=1, source_target_pairs={{0,1},{1,32},{32,33},{33,2},{2,3},{3,34},{34,35},{35,4},{4,5},{5,3... | collective-permute-start | bytes 786440 | tf_op jit(solution)/shard_map/ppermute | solution.py:34
  355.6 5.2 %conv_second.11.acc_ref = f32[2,256,512]{2,1,0:T(8,128)S(1)} custom-call(bf16[2,256,512]{2,1,0:T(8,128)(2,1)S(1)} %conv_first.11.a_ref, bf16[12,1024,512]{2,1,0:T(8,128)(2,1)S(1)} %bitcast.81), custom_call_target="tpu_custom_call" | custom-call | flops 2952790016 | bytes 7340032 | tf_op jit(solution)/shard_map/conv_second/pallas_call | solution.py:179
  362.3 1.3 collective-permute-start.18
  364.3 4.5 conv_first.12.a_ref
  368.9 3.6 collective-permute-start.12
  373.8 5.2 %conv_second.12.acc_ref = f32[2,256,512]{2,1,0:T(8,128)S(1)} custom-call(bf16[2,256,512]{2,1,0:T(8,128)(2,1)S(1)} %conv_first.12.a_ref, bf16[12,1024,512]{2,1,0:T(8,128)(2,1)S(1)} %bitcast.81), custom_call_target="tpu_custom_call" | custom-call | flops 2952790016 | bytes 7340032 | tf_op jit(solution)/shard_map/conv_second/pallas_call | solution.py:179
  379.8 4.5 conv_first.13.a_ref
  384.4 3.7 collective-permute-start.15
  388.1 1.5 collective-permute-start.16
  389.6 5.2 %conv_second.13.acc_ref = f32[2,256,512]{2,1,0:T(8,128)S(1)} custom-call(bf16[2,256,512]{2,1,0:T(8,128)(2,1)S(1)} %conv_first.13.a_ref, bf16[12,1024,512]{2,1,0:T(8,128)(2,1)S(1)} %bitcast.81), custom_call_target="tpu_custom_call" | custom-call | flops 2952790016 | bytes 7340032 | tf_op jit(solution)/shard_map/conv_second/pallas_call | solution.py:179
  396.3 4.5 conv_first.14.a_ref
  400.9 4.0 collective-permute-start.19
  404.9 1.3 collective-permute-start.20
  406.2 5.2 %conv_second.14.acc_ref = f32[2,256,512]{2,1,0:T(8,128)S(1)} custom-call(bf16[2,256,512]{2,1,0:T(8,128)(2,1)S(1)} %conv_first.14.a_ref, bf16[12,1024,512]{2,1,0:T(8,128)(2,1)S(1)} %bitcast.81), custom_call_target="tpu_custom_call" | custom-call | flops 2952790016 | bytes 7340032 | tf_op jit(solution)/shard_map/conv_second/pallas_call | solution.py:179
  412.2 4.5 conv_first.15.a_ref
  416.8 4.5 collective-permute-start.21
  421.3 1.3 collective-permute-start.22
  422.6 5.2 %conv_second.15.acc_ref = f32[2,256,512]{2,1,0:T(8,128)S(1)} custom-call(bf16[2,256,512]{2,1,0:T(8,128)(2,1)S(1)} %conv_first.15.a_ref, bf16[12,1024,512]{2,1,0:T(8,128)(2,1)S(1)} %bitcast.81), custom_call_target="tpu_custom_call" | custom-call | flops 2952790016 | bytes 7340032 | tf_op jit(solution)/shard_map/conv_second/pallas_call | solution.py:179
  429.8 1.3 collective-permute-start.25
  431.1 33.0 %collective-permute-done.25 = bf16[2,2,2,16,512]{4,3,2,1,0:T(8,128)(2,1)S(1)} collective-permute-done((bf16[2,2,2,16,512]{4,3,2,1,0:T(8,128)(2,1)S(1)}, bf16[2,2,2,16,512]{4,3,2,1,0:T(8,128)(2,1)S(1)}, u32[]{:S(2)}, u32[]{:S(2)}) %collective-permute-start.25) | collective-permute-done | bytes 131104 | tf_op jit(solution)/shard_map/ppermute | solution.py:34
  464.2 7.3 %collective-permute-start.26 = (bf16[2,16,512]{2,1,0:T(8,128)(2,1)S(1)}, bf16[2,16,512]{2,1,0:T(8,128)(2,1)S(1)}, u32[]{:S(2)}, u32[]{:S(2)}) collective-permute-start(bf16[2,16,512]{2,1,0:T(8,128)(2,1)S(1)} %get-tuple-element.32), channel_id=1, source_target_pairs={{0,0},{1,2},{32,4},{33,6},{2,8},{3,10},{34,12},{35,14},{4,16},{5,1... | collective-permute-start | bytes 98312 | tf_op jit(solution)/shard_map/ppermute | solution.py:34
  471.6 9.8 %collective-permute-start.28 = (bf16[2,16,512]{2,1,0:T(8,128)(2,1)S(1)}, bf16[2,16,512]{2,1,0:T(8,128)(2,1)S(1)}, u32[]{:S(2)}, u32[]{:S(2)}) collective-permute-start(bf16[2,16,512]{2,1,0:T(8,128)(2,1)S(1)} %get-tuple-element.34), channel_id=1, source_target_pairs={{0,1},{1,3},{32,5},{33,7},{2,9},{3,11},{34,13},{35,15},{4,17},{5,1... | collective-permute-start | bytes 98312 | tf_op jit(solution)/shard_map/ppermute | solution.py:34
  481.4 1.9 collective-permute-start.29
  483.4 7.1 %collective-permute-done.29 = bf16[2,16,512]{2,1,0:T(8,128)(2,1)S(1)} collective-permute-done((bf16[2,16,512]{2,1,0:T(8,128)(2,1)S(1)}, bf16[2,16,512]{2,1,0:T(8,128)(2,1)S(1)}, u32[]{:S(2)}, u32[]{:S(2)}) %collective-permute-start.29) | collective-permute-done | bytes 32800 | tf_op jit(solution)/shard_map/ppermute | solution.py:34
  (77 shorter events, 13.3 us)
Async XLA Ops:
  6.5 157.7 %all-gather.6.cloned.1.call-start = ((), (), s32[]{:S(2)}) async-start(), calls=%async_computation.1 | async-start | bytes 9584640 | tf_op jit(solution)/shard_map/all_gather | solution.py:255
  7.3 282.2 %all-gather.4.cloned.1.call-start = ((), (), s32[]{:S(2)}) async-start(), calls=%async_computation | async-start | bytes 12779520 | tf_op jit(solution)/shard_map/all_gather | solution.py:257
  10.0 11.8 %collective-permute-start = (bf16[256,512]{1,0:T(8,128)(2,1)S(1)}, bf16[256,512]{1,0:T(8,128)(2,1)S(1)}, u32[]{:S(2)}, u32[]{:S(2)}) collective-permute-start(bf16[256,512]{1,0:T(8,128)(2,1)S(1)} %get-tuple-element.5), channel_id=1, source_target_pairs={{0,0},{1,8},{32,16},{33,24},{2,1},{3,9},{34,17},{35,25},{4,32},{5,... | collective-permute-start | bytes 786440 | tf_op jit(solution)/shard_map/ppermute | solution.py:34
  15.2 11.9 %collective-permute-start.1 = (bf16[256,512]{1,0:T(8,128)(2,1)S(1)}, bf16[256,512]{1,0:T(8,128)(2,1)S(1)}, u32[]{:S(2)}, u32[]{:S(2)}) collective-permute-start(bf16[256,512]{1,0:T(8,128)(2,1)S(1)} %get-tuple-element.6), channel_id=1, source_target_pairs={{0,8},{1,0},{32,24},{33,16},{2,9},{3,1},{34,25},{35,17},{4,40},{5,... | collective-permute-start | bytes 786440 | tf_op jit(solution)/shard_map/ppermute | solution.py:34
  164.2 3.7 copy-start.1
  172.5 126.7 %collective-permute-start.2 = (bf16[256,512]{1,0:T(8,128)(2,1)S(1)}, bf16[256,512]{1,0:T(8,128)(2,1)S(1)}, u32[]{:S(2)}, u32[]{:S(2)}) collective-permute-start(bf16[256,512]{1,0:T(8,128)(2,1)S(1)} %get-tuple-element.25), channel_id=1, source_target_pairs={{0,1},{1,32},{32,33},{33,2},{2,3},{3,34},{34,35},{35,4},{4,5},{5,3... | collective-permute-start | bytes 786440 | tf_op jit(solution)/shard_map/ppermute | solution.py:34
  174.7 124.5 %collective-permute-start.3 = (bf16[256,512]{1,0:T(8,128)(2,1)S(1)}, bf16[256,512]{1,0:T(8,128)(2,1)S(1)}, u32[]{:S(2)}, u32[]{:S(2)}) collective-permute-start(bf16[256,512]{1,0:T(8,128)(2,1)S(1)} %get-tuple-element.24), channel_id=1, source_target_pairs={{1,0},{32,1},{33,32},{2,33},{3,2},{34,3},{35,34},{4,35},{5,4},{36,... | collective-permute-start | bytes 786440 | tf_op jit(solution)/shard_map/ppermute | solution.py:34
  289.4 4.6 copy-start
  294.0 5.8 %copy-start.2 = (bf16[1,9,1024,512]{3,2,1,0:T(8,128)(2,1)S(1)}, bf16[1,9,1024,512]{3,2,1,0:T(8,128)(2,1)}, u32[]{:S(2)}) copy-start(bf16[1,9,1024,512]{3,2,1,0:T(8,128)(2,1)} %all-gather.6.cloned.1.call-done) | copy-start | bytes 28311556
  299.2 8.7 %slice-start = ((s8[12582912]{0:T(1024)(128)(4,1)}), s8[4194304]{0:T(1024)(128)(4,1)S(1)}, s32[]{:S(2)}) async-start(s8[12582912]{0:T(1024)(128)(4,1)} %bitcast.80), calls=%async_computation.2 | async-start | bytes 8388608
  299.2 8.7 %slice-start.1 = ((s8[12582912]{0:T(1024)(128)(4,1)}), s8[4194304]{0:T(1024)(128)(4,1)S(1)}, s32[]{:S(2)}) async-start(s8[12582912]{0:T(1024)(128)(4,1)} %bitcast.80), calls=%async_computation.3 | async-start | bytes 8388608
  299.8 8.1 %slice-start.2 = ((s8[12582912]{0:T(1024)(128)(4,1)}), s8[4194304]{0:T(1024)(128)(4,1)S(1)}, s32[]{:S(2)}) async-start(s8[12582912]{0:T(1024)(128)(4,1)} %bitcast.80), calls=%async_computation.4 | async-start | bytes 8388608
  304.4 8.7 %collective-permute-start.4 = (bf16[256,512]{1,0:T(8,128)(2,1)S(1)}, bf16[256,512]{1,0:T(8,128)(2,1)S(1)}, u32[]{:S(2)}, u32[]{:S(2)}) collective-permute-start(bf16[256,512]{1,0:T(8,128)(2,1)S(1)} %get-tuple-element.23), channel_id=1, source_target_pairs={{0,1},{1,32},{32,33},{33,2},{2,3},{3,34},{34,35},{35,4},{4,5},{5,3... | collective-permute-start | bytes 786440 | tf_op jit(solution)/shard_map/ppermute | solution.py:34
  306.6 6.5 %collective-permute-start.5 = (bf16[256,512]{1,0:T(8,128)(2,1)S(1)}, bf16[256,512]{1,0:T(8,128)(2,1)S(1)}, u32[]{:S(2)}, u32[]{:S(2)}) collective-permute-start(bf16[256,512]{1,0:T(8,128)(2,1)S(1)} %get-tuple-element.22), channel_id=1, source_target_pairs={{1,0},{32,1},{33,32},{2,33},{3,2},{34,3},{35,34},{4,35},{5,4},{36,... | collective-permute-start | bytes 786440 | tf_op jit(solution)/shard_map/ppermute | solution.py:34
  313.7 13.2 %collective-permute-start.6 = (bf16[2,256,512]{2,1,0:T(8,128)(2,1)S(1)}, bf16[2,256,512]{2,1,0:T(8,128)(2,1)S(1)}, u32[]{:S(2)}, u32[]{:S(2)}) collective-permute-start(bf16[2,256,512]{2,1,0:T(8,128)(2,1)S(1)} %halo_and_residual.9), channel_id=1, source_target_pairs={{0,64},{1,65},{32,96},{33,97},{2,66},{3,67},{34,98},{35,99},{4,68}... | collective-permute-start | bytes 1572872 | tf_op jit(solution)/shard_map/ppermute | solution.py:34
  331.5 10.9 %collective-permute-start.7 = (bf16[256,512]{1,0:T(8,128)(2,1)S(1)}, bf16[256,512]{1,0:T(8,128)(2,1)S(1)}, u32[]{:S(2)}, u32[]{:S(2)}) collective-permute-start(bf16[256,512]{1,0:T(8,128)(2,1)S(1)} %get-tuple-element.21), channel_id=1, source_target_pairs={{0,1},{1,32},{32,33},{33,2},{2,3},{3,34},{34,35},{35,4},{4,5},{5,3... | collective-permute-start | bytes 786440 | tf_op jit(solution)/shard_map/ppermute | solution.py:34
  335.7 6.7 %collective-permute-start.8 = (bf16[256,512]{1,0:T(8,128)(2,1)S(1)}, bf16[256,512]{1,0:T(8,128)(2,1)S(1)}, u32[]{:S(2)}, u32[]{:S(2)}) collective-permute-start(bf16[256,512]{1,0:T(8,128)(2,1)S(1)} %get-tuple-element.20), channel_id=1, source_target_pairs={{1,0},{32,1},{33,32},{2,33},{3,2},{34,3},{35,34},{4,35},{5,4},{36,... | collective-permute-start | bytes 786440 | tf_op jit(solution)/shard_map/ppermute | solution.py:34
  347.6 13.2 %collective-permute-start.10 = (bf16[256,512]{1,0:T(8,128)(2,1)S(1)}, bf16[256,512]{1,0:T(8,128)(2,1)S(1)}, u32[]{:S(2)}, u32[]{:S(2)}) collective-permute-start(bf16[256,512]{1,0:T(8,128)(2,1)S(1)} %get-tuple-element.18), channel_id=1, source_target_pairs={{1,0},{32,1},{33,32},{2,33},{3,2},{34,3},{35,34},{4,35},{5,4},{36,... | collective-permute-start | bytes 786440 | tf_op jit(solution)/shard_map/ppermute | solution.py:34
  348.9 11.9 %collective-permute-start.9 = (bf16[256,512]{1,0:T(8,128)(2,1)S(1)}, bf16[256,512]{1,0:T(8,128)(2,1)S(1)}, u32[]{:S(2)}, u32[]{:S(2)}) collective-permute-start(bf16[256,512]{1,0:T(8,128)(2,1)S(1)} %get-tuple-element.19), channel_id=1, source_target_pairs={{0,1},{1,32},{32,33},{33,2},{2,3},{3,34},{34,35},{35,4},{4,5},{5,3... | collective-permute-start | bytes 786440 | tf_op jit(solution)/shard_map/ppermute | solution.py:34
  361.6 2.7 collective-permute-start.11
  362.3 33.8 %collective-permute-start.18 = (bf16[2,256,512]{2,1,0:T(8,128)(2,1)S(1)}, bf16[2,256,512]{2,1,0:T(8,128)(2,1)S(1)}, u32[]{:S(2)}, u32[]{:S(2)}) collective-permute-start(bf16[2,256,512]{2,1,0:T(8,128)(2,1)S(1)} %halo_and_residual.8.e_ref), channel_id=1, source_target_pairs={{0,192},{1,193},{32,224},{33,225},{2,194},{3,195},{34,226},{35,227... | collective-permute-start | bytes 1572872 | tf_op jit(solution)/shard_map/ppermute | solution.py:34
  363.6 16.1 %collective-permute-start.14 = (bf16[2,256,512]{2,1,0:T(8,128)(2,1)S(1)}, bf16[2,256,512]{2,1,0:T(8,128)(2,1)S(1)}, u32[]{:S(2)}, u32[]{:S(2)}) collective-permute-start(bf16[2,256,512]{2,1,0:T(8,128)(2,1)S(1)} %collective-permute-done.6.e_ref), channel_id=1, source_target_pairs={{64,128},{65,129},{96,160},{97,161},{66,130},{67,131},{98,162},{99... | collective-permute-start | bytes 1572872 | tf_op jit(solution)/shard_map/ppermute | solution.py:34
  368.9 10.1 %collective-permute-start.12 = (bf16[256,512]{1,0:T(8,128)(2,1)S(1)}, bf16[256,512]{1,0:T(8,128)(2,1)S(1)}, u32[]{:S(2)}, u32[]{:S(2)}) collective-permute-start(bf16[256,512]{1,0:T(8,128)(2,1)S(1)} %get-tuple-element.17), channel_id=1, source_target_pairs={{0,1},{1,32},{32,33},{33,2},{2,3},{3,34},{34,35},{35,4},{4,5},{5,3... | collective-permute-start | bytes 786440 | tf_op jit(solution)/shard_map/ppermute | solution.py:34
  372.5 6.5 %collective-permute-start.13 = (bf16[256,512]{1,0:T(8,128)(2,1)S(1)}, bf16[256,512]{1,0:T(8,128)(2,1)S(1)}, u32[]{:S(2)}, u32[]{:S(2)}) collective-permute-start(bf16[256,512]{1,0:T(8,128)(2,1)S(1)} %get-tuple-element.16), channel_id=1, source_target_pairs={{1,0},{32,1},{33,32},{2,33},{3,2},{34,3},{35,34},{4,35},{5,4},{36,... | collective-permute-start | bytes 786440 | tf_op jit(solution)/shard_map/ppermute | solution.py:34
  384.4 10.4 %collective-permute-start.15 = (bf16[256,512]{1,0:T(8,128)(2,1)S(1)}, bf16[256,512]{1,0:T(8,128)(2,1)S(1)}, u32[]{:S(2)}, u32[]{:S(2)}) collective-permute-start(bf16[256,512]{1,0:T(8,128)(2,1)S(1)} %get-tuple-element.15), channel_id=1, source_target_pairs={{0,1},{1,32},{32,33},{33,2},{2,3},{3,34},{34,35},{35,4},{4,5},{5,3... | collective-permute-start | bytes 786440 | tf_op jit(solution)/shard_map/ppermute | solution.py:34
  388.1 6.7 %collective-permute-start.16 = (bf16[256,512]{1,0:T(8,128)(2,1)S(1)}, bf16[256,512]{1,0:T(8,128)(2,1)S(1)}, u32[]{:S(2)}, u32[]{:S(2)}) collective-permute-start(bf16[256,512]{1,0:T(8,128)(2,1)S(1)} %get-tuple-element.14), channel_id=1, source_target_pairs={{1,0},{32,1},{33,32},{2,33},{3,2},{34,3},{35,34},{4,35},{5,4},{36,... | collective-permute-start | bytes 786440 | tf_op jit(solution)/shard_map/ppermute | solution.py:34
  395.4 0.7 collective-permute-start.17
  400.9 10.5 %collective-permute-start.19 = (bf16[256,512]{1,0:T(8,128)(2,1)S(1)}, bf16[256,512]{1,0:T(8,128)(2,1)S(1)}, u32[]{:S(2)}, u32[]{:S(2)}) collective-permute-start(bf16[256,512]{1,0:T(8,128)(2,1)S(1)} %get-tuple-element.13), channel_id=1, source_target_pairs={{0,1},{1,32},{32,33},{33,2},{2,3},{3,34},{34,35},{35,4},{4,5},{5,3... | collective-permute-start | bytes 786440 | tf_op jit(solution)/shard_map/ppermute | solution.py:34
  404.9 6.5 %collective-permute-start.20 = (bf16[256,512]{1,0:T(8,128)(2,1)S(1)}, bf16[256,512]{1,0:T(8,128)(2,1)S(1)}, u32[]{:S(2)}, u32[]{:S(2)}) collective-permute-start(bf16[256,512]{1,0:T(8,128)(2,1)S(1)} %get-tuple-element.12), channel_id=1, source_target_pairs={{1,0},{32,1},{33,32},{2,33},{3,2},{34,3},{35,34},{4,35},{5,4},{36,... | collective-permute-start | bytes 786440 | tf_op jit(solution)/shard_map/ppermute | solution.py:34
  416.8 11.0 %collective-permute-start.21 = (bf16[256,512]{1,0:T(8,128)(2,1)S(1)}, bf16[256,512]{1,0:T(8,128)(2,1)S(1)}, u32[]{:S(2)}, u32[]{:S(2)}) collective-permute-start(bf16[256,512]{1,0:T(8,128)(2,1)S(1)} %get-tuple-element.11), channel_id=1, source_target_pairs={{0,1},{1,32},{32,33},{33,2},{2,3},{3,34},{34,35},{35,4},{4,5},{5,3... | collective-permute-start | bytes 786440 | tf_op jit(solution)/shard_map/ppermute | solution.py:34
  421.3 6.5 %collective-permute-start.22 = (bf16[256,512]{1,0:T(8,128)(2,1)S(1)}, bf16[256,512]{1,0:T(8,128)(2,1)S(1)}, u32[]{:S(2)}, u32[]{:S(2)}) collective-permute-start(bf16[256,512]{1,0:T(8,128)(2,1)S(1)} %get-tuple-element.10), channel_id=1, source_target_pairs={{1,0},{32,1},{33,32},{2,33},{3,2},{34,3},{35,34},{4,35},{5,4},{36,... | collective-permute-start | bytes 786440 | tf_op jit(solution)/shard_map/ppermute | solution.py:34
  428.4 2.7 collective-permute-start.23
  429.1 2.0 collective-permute-start.24
  429.8 34.3 %collective-permute-start.25 = (bf16[2,2,2,16,512]{4,3,2,1,0:T(8,128)(2,1)S(1)}, bf16[2,2,2,16,512]{4,3,2,1,0:T(8,128)(2,1)S(1)}, u32[]{:S(2)}, u32[]{:S(2)}) collective-permute-start(bf16[2,2,2,16,512]{4,3,2,1,0:T(8,128)(2,1)S(1)} %get-tuple-element.7), channel_id=1, source_target_pairs={{192,0},{193,1},{224,32},{225,33},{194,2},{195,3},{226,34},{227,35... | collective-permute-start | bytes 393224 | tf_op jit(solution)/shard_map/ppermute | solution.py:34
  464.2 19.2 %collective-permute-start.26 = (bf16[2,16,512]{2,1,0:T(8,128)(2,1)S(1)}, bf16[2,16,512]{2,1,0:T(8,128)(2,1)S(1)}, u32[]{:S(2)}, u32[]{:S(2)}) collective-permute-start(bf16[2,16,512]{2,1,0:T(8,128)(2,1)S(1)} %get-tuple-element.32), channel_id=1, source_target_pairs={{0,0},{1,2},{32,4},{33,6},{2,8},{3,10},{34,12},{35,14},{4,16},{5,1... | collective-permute-start | bytes 98312 | tf_op jit(solution)/shard_map/ppermute | solution.py:34
  471.5 11.9 %collective-permute-start.27 = (bf16[2,16,512]{2,1,0:T(8,128)(2,1)S(1)}, bf16[2,16,512]{2,1,0:T(8,128)(2,1)S(1)}, u32[]{:S(2)}, u32[]{:S(2)}) collective-permute-start(bf16[2,16,512]{2,1,0:T(8,128)(2,1)S(1)} %get-tuple-element.35), channel_id=1, source_target_pairs={{0,32},{1,34},{32,36},{33,38},{2,40},{3,42},{34,44},{35,46},{4,48}... | collective-permute-start | bytes 98312 | tf_op jit(solution)/shard_map/ppermute | solution.py:34
  471.6 11.8 %collective-permute-start.28 = (bf16[2,16,512]{2,1,0:T(8,128)(2,1)S(1)}, bf16[2,16,512]{2,1,0:T(8,128)(2,1)S(1)}, u32[]{:S(2)}, u32[]{:S(2)}) collective-permute-start(bf16[2,16,512]{2,1,0:T(8,128)(2,1)S(1)} %get-tuple-element.34), channel_id=1, source_target_pairs={{0,1},{1,3},{32,5},{33,7},{2,9},{3,11},{34,13},{35,15},{4,17},{5,1... | collective-permute-start | bytes 98312 | tf_op jit(solution)/shard_map/ppermute | solution.py:34
  481.4 9.1 %collective-permute-start.29 = (bf16[2,16,512]{2,1,0:T(8,128)(2,1)S(1)}, bf16[2,16,512]{2,1,0:T(8,128)(2,1)S(1)}, u32[]{:S(2)}, u32[]{:S(2)}) collective-permute-start(bf16[2,16,512]{2,1,0:T(8,128)(2,1)S(1)} %get-tuple-element.33), channel_id=1, source_target_pairs={{0,33},{1,35},{32,37},{33,39},{2,41},{3,43},{34,45},{35,47},{4,49}... | collective-permute-start | bytes 98312 | tf_op jit(solution)/shard_map/ppermute | solution.py:34
Sparse Core Ops, SparseCore 0:
  9.2 154.9 all-gather.5
  166.1 123.2 all-gather.3
